TPU v7x, 256 devices: a whole 4x4x8 slice. The times are simulated.
256 devices in a mesh: depth: 32 (over z, x), tile: 8 (over y, core).
Axes of the slice: x: 4, y: 4, z: 8, core: 2. Of those that a mesh axis runs over, the one named last changes fastest.
Arguments:
- tidal: float32 [32, 3, 131072], P('depth', None, 'tile'), may hold values from -1.5 to 1.5
- plane_weight: float32 [32], P('depth'), may hold values from 0.2 to 1
- plane_step: float32 [32], P('depth'), may hold values from 0.2 to 0.6
- ray_angle: float32 [131072], P('tile'), may hold values from -3.140625 to 3.140625
- dest_tile: int32 [32, 1024, 1], P('depth', 'tile'), may hold values from 0 to 7; in each aligned block of 128 rows (0 to 127, 128 to 255, ..., all dimensions but the last counted through in order) at most 32 rows name the same one
- dest_segment: int32 [32, 1024], P('depth', 'tile'), may hold values from 0 to 255
- interp: bfloat16 [32, 1024, 128, 128], P('depth', 'tile'), may hold values from -0.5 to 0.5
Outputs:
- potential_adjoint: float32 [32, 16, 16384], P('depth', 'tile')
Inputs may be any that keep to these rules, and one draw needn't show every extreme that they name: `dest_tile`: in each plane, the 128 blocks of one strip name no strip more than 32 times, a bound that some block reaches.
All inputs are finite; a program needn't handle non-finite values.
Results may differ from a plain program's by a relative error of at most 0.003.
Values sent between devices are 32-bit elements; how exact they have to be, the bound alone decides.
A program may use at most 64 MiB of HBM per device.

v0:
```python
import jax
import jax.numpy as jnp
from jax import lax
from jax.sharding import PartitionSpec as P

ROWS = 2
COLS = 16384


def from_behind(value, axis, steps):
    count = lax.axis_size(axis)
    leading, last = (max(0, -steps), min(count, count - steps))
    return lax.ppermute(value, axis, [(source, source + steps) for source in range(leading, last)])


def padded_2(shard, sides, width):
    for axis, dim in sides:
        count, length = (lax.axis_size(axis), shard.shape[dim])
        up = [(i, (i + 1) % count) for i in range(count - 1)]
        down = [(j, i) for i, j in up]
        last = lax.slice_in_dim(shard, length - width, length, axis=dim)
        leading = lax.slice_in_dim(shard, 0, width, axis=dim)
        before = lax.ppermute(last, axis, up)
        after = lax.ppermute(leading, axis, down)
        shard = jnp.concatenate([before, shard, after], axis=dim)
    return shard


def column_part(field):
    padded = jnp.pad(field, ((0, 0), (0, 0), (1, 1)))
    return 0.5 * (padded[:, :, :-2] - padded[:, :, 2:])


def smooth_cols(field):
    padded = jnp.pad(field, ((0, 0), (0, 0), (1, 1)))
    return 0.25 * padded[:, :, :-2] + 0.5 * field + 0.25 * padded[:, :, 2:]


def per_device(tidal, plane_weight, plane_step, ray_angle, dest_tile, dest_segment, interp):
    planes_here = tidal.shape[0]
    n_tile = lax.axis_size("tile")
    n_depth = lax.axis_size("depth")
    blocks_here = interp.shape[1]
    width = interp.shape[2]
    slots = 2 * blocks_here // n_tile
    segments = ROWS * COLS // width
    jxx = tidal[:, 0]
    jxy = tidal[:, 1]
    jyy = tidal[:, 2]
    local_terms = jnp.stack(
        [
            -jnp.sum(plane_weight[:, None] * (jxx - jyy) * 0.5, axis=0),
            -jnp.sum(plane_weight[:, None] * jxy, axis=0),
        ]
    )
    shear = lax.psum(local_terms, "depth")
    cross = -shear[0] * jnp.sin(2.0 * ray_angle) + shear[1] * jnp.cos(2.0 * ray_angle)
    seed_state = jnp.stack(
        [
            cross * jnp.cos(ray_angle),
            cross * jnp.sin(ray_angle),
            jnp.zeros_like(cross),
            jnp.zeros_like(cross),
        ]
    )

    def sweep(top):
        xb_one, xb_two, tb_one, tb_two = (top[0], top[1], top[2], top[3])
        step_len = plane_step[0]
        tp_one = tb_one + step_len * xb_one
        tp_two = tb_two + step_len * xb_two
        adjoints = [jnp.stack([-tp_one, -tp_two])]
        new_one = xb_one - (jxx[0] * tp_one + jxy[0] * tp_two)
        new_two = xb_two - (jxy[0] * tp_one + jyy[0] * tp_two)
        return (jnp.stack([new_one, new_two, tp_one, tp_two]), jnp.stack(adjoints[::-1]))

    is_last = lax.axis_index("depth") == n_depth - 1

    def relay_step(turn, top):
        bottom, unused = sweep(top)
        incoming = from_behind(bottom, "depth", -1)
        return jnp.where(is_last, seed_state, incoming)

    top_state = lax.fori_loop(0, n_depth - 1, relay_step, seed_state)
    unused_state, deflection_bar = sweep(top_state)
    abar = deflection_bar.astype(jnp.bfloat16).reshape(planes_here, 2, blocks_here, width)
    contrib = jnp.einsum("pcbr,pbrk->pbck", abar, interp, preferred_element_type=jnp.float32)
    dest = dest_tile[:, :, 0]
    order_mask = jnp.arange(blocks_here)[None, :] < jnp.arange(blocks_here)[:, None]
    same_dest = dest[:, :, None] == dest[:, None, :]
    rank = jnp.sum(jnp.logical_and(same_dest, order_mask[None]), axis=2)
    slot = dest[0] * slots + rank[0]
    send_data = jnp.zeros((n_tile * slots, 2, width), jnp.float32).at[slot].set(contrib[0])
    send_ids = jnp.zeros((n_tile * slots,), jnp.int32).at[slot].set(dest_segment[0])
    got_data = lax.all_to_all(
        send_data.reshape(n_tile, slots, 2, width), "tile", split_axis=0, concat_axis=0, tiled=True
    )
    got_ids = lax.all_to_all(
        send_ids.reshape(n_tile, slots), "tile", split_axis=0, concat_axis=0, tiled=True
    )
    summed = (
        jnp.zeros((segments, 2, width), jnp.float32)
        .at[got_ids.reshape(-1)]
        .add(got_data.reshape(-1, 2, width))
    )
    plane_maps = [jnp.transpose(summed, (1, 0, 2)).reshape(2, ROWS, COLS)]
    maps = jnp.stack(plane_maps)
    ay_ext = padded_2(maps[:, 1], (("tile", 1),), 1)
    raw = column_part(maps[:, 0]) + 0.5 * (ay_ext[:, :-2, :] - ay_ext[:, 2:, :])
    raw_ext = padded_2(raw, (("tile", 1),), 1)
    rows_done = 0.25 * raw_ext[:, :-2, :] + 0.5 * raw_ext[:, 1:-1, :] + 0.25 * raw_ext[:, 2:, :]
    return smooth_cols(rows_done)


def solution(mesh):
    return jax.shard_map(
        per_device,
        mesh=mesh,
        in_specs=(
            P("depth", None, "tile"),
            P("depth"),
            P("depth"),
            P("tile"),
            P("depth", "tile", None),
            P("depth", "tile"),
            P("depth", "tile", None, None),
        ),
        out_specs=P("depth", "tile", None),
        check_vma=False,
    )
```

profile of v0, /device:TPU:103, one launch (start us, length us, event | category | flops | bytes accessed | tf_op | source)
XLA Modules:
  0.0 640.3 jit_solution(10379709504389961642)
XLA Ops:
  19.2 129.9 %all-reduce.4.cloned.1.call-done = f32[2,16384]{1,0:T(2,128)} async-done(((f32[2,16384]{1,0:T(2,128)}), f32[2,16384]{1,0:T(2,128)}) %all-reduce.4.cloned.1.call-update) | async-done | bytes 131088 | tf_op jit(solution)/shard_map/psum | solution.py:56
  151.7 387.7 %while.10 = (s32[]{:T(128)}, f32[4,16384]{1,0:T(4,128)S(1)}, pred[]{:T(512)}, f32[1,1,16384]{2,1,0:T(1,128)S(1)}, f32[1]{0:T(128)}, /*index=5*/f32[1,1,16384]{2,...) while((s32[]{:T(128)}, f32[4,16384]{1,0:T(4,128)S(1)}, pred[]{:T(512)}, ...), condition=%wide.region_4.5_spmd, body=%wide.region_3.4_spmd.sunk | while | flops 458754 | bytes 3342474 | solution.py:84
  166.8 8.5 %collective-permute-done = f32[4,16384]{1,0:T(4,128)S(1)} collective-permute-done((f32[4,16384]{1,0:T(4,128)S(1)}, f32[4,16384]{1,0:T(4,128)S(1)}, u32[]{:S(2)}, u32[]{:S(2)}) %collective-permute-start) | collective-permute-done | bytes 262176 | tf_op jit(solution)/shard_map/while/body/eval_jaxpr/ppermute | solution.py:13
  178.7 8.5 %collective-permute-done = f32[4,16384]{1,0:T(4,128)S(1)} collective-permute-done((f32[4,16384]{1,0:T(4,128)S(1)}, f32[4,16384]{1,0:T(4,128)S(1)}, u32[]{:S(2)}, u32[]{:S(2)}) %collective-permute-start) | collective-permute-done | bytes 262176 | tf_op jit(solution)/shard_map/while/body/eval_jaxpr/ppermute | solution.py:13
  202.4 8.7 %collective-permute-done = f32[4,16384]{1,0:T(4,128)S(1)} collective-permute-done((f32[4,16384]{1,0:T(4,128)S(1)}, f32[4,16384]{1,0:T(4,128)S(1)}, u32[]{:S(2)}, u32[]{:S(2)}) %collective-permute-start) | collective-permute-done | bytes 262176 | tf_op jit(solution)/shard_map/while/body/eval_jaxpr/ppermute | solution.py:13
  214.5 9.9 %collective-permute-done = f32[4,16384]{1,0:T(4,128)S(1)} collective-permute-done((f32[4,16384]{1,0:T(4,128)S(1)}, f32[4,16384]{1,0:T(4,128)S(1)}, u32[]{:S(2)}, u32[]{:S(2)}) %collective-permute-start) | collective-permute-done | bytes 262176 | tf_op jit(solution)/shard_map/while/body/eval_jaxpr/ppermute | solution.py:13
  227.7 11.0 %collective-permute-done = f32[4,16384]{1,0:T(4,128)S(1)} collective-permute-done((f32[4,16384]{1,0:T(4,128)S(1)}, f32[4,16384]{1,0:T(4,128)S(1)}, u32[]{:S(2)}, u32[]{:S(2)}) %collective-permute-start) | collective-permute-done | bytes 262176 | tf_op jit(solution)/shard_map/while/body/eval_jaxpr/ppermute | solution.py:13
  242.0 10.8 %collective-permute-done = f32[4,16384]{1,0:T(4,128)S(1)} collective-permute-done((f32[4,16384]{1,0:T(4,128)S(1)}, f32[4,16384]{1,0:T(4,128)S(1)}, u32[]{:S(2)}, u32[]{:S(2)}) %collective-permute-start) | collective-permute-done | bytes 262176 | tf_op jit(solution)/shard_map/while/body/eval_jaxpr/ppermute | solution.py:13
  256.1 9.9 %collective-permute-done = f32[4,16384]{1,0:T(4,128)S(1)} collective-permute-done((f32[4,16384]{1,0:T(4,128)S(1)}, f32[4,16384]{1,0:T(4,128)S(1)}, u32[]{:S(2)}, u32[]{:S(2)}) %collective-permute-start) | collective-permute-done | bytes 262176 | tf_op jit(solution)/shard_map/while/body/eval_jaxpr/ppermute | solution.py:13
  269.4 9.1 %collective-permute-done = f32[4,16384]{1,0:T(4,128)S(1)} collective-permute-done((f32[4,16384]{1,0:T(4,128)S(1)}, f32[4,16384]{1,0:T(4,128)S(1)}, u32[]{:S(2)}, u32[]{:S(2)}) %collective-permute-start) | collective-permute-done | bytes 262176 | tf_op jit(solution)/shard_map/while/body/eval_jaxpr/ppermute | solution.py:13
  281.8 8.5 %collective-permute-done = f32[4,16384]{1,0:T(4,128)S(1)} collective-permute-done((f32[4,16384]{1,0:T(4,128)S(1)}, f32[4,16384]{1,0:T(4,128)S(1)}, u32[]{:S(2)}, u32[]{:S(2)}) %collective-permute-start) | collective-permute-done | bytes 262176 | tf_op jit(solution)/shard_map/while/body/eval_jaxpr/ppermute | solution.py:13
  293.7 8.5 %collective-permute-done = f32[4,16384]{1,0:T(4,128)S(1)} collective-permute-done((f32[4,16384]{1,0:T(4,128)S(1)}, f32[4,16384]{1,0:T(4,128)S(1)}, u32[]{:S(2)}, u32[]{:S(2)}) %collective-permute-start) | collective-permute-done | bytes 262176 | tf_op jit(solution)/shard_map/while/body/eval_jaxpr/ppermute | solution.py:13
  317.4 8.5 %collective-permute-done = f32[4,16384]{1,0:T(4,128)S(1)} collective-permute-done((f32[4,16384]{1,0:T(4,128)S(1)}, f32[4,16384]{1,0:T(4,128)S(1)}, u32[]{:S(2)}, u32[]{:S(2)}) %collective-permute-start) | collective-permute-done | bytes 262176 | tf_op jit(solution)/shard_map/while/body/eval_jaxpr/ppermute | solution.py:13
  353.0 8.6 %collective-permute-done = f32[4,16384]{1,0:T(4,128)S(1)} collective-permute-done((f32[4,16384]{1,0:T(4,128)S(1)}, f32[4,16384]{1,0:T(4,128)S(1)}, u32[]{:S(2)}, u32[]{:S(2)}) %collective-permute-start) | collective-permute-done | bytes 262176 | tf_op jit(solution)/shard_map/while/body/eval_jaxpr/ppermute | solution.py:13
  365.0 9.8 %collective-permute-done = f32[4,16384]{1,0:T(4,128)S(1)} collective-permute-done((f32[4,16384]{1,0:T(4,128)S(1)}, f32[4,16384]{1,0:T(4,128)S(1)}, u32[]{:S(2)}, u32[]{:S(2)}) %collective-permute-start) | collective-permute-done | bytes 262176 | tf_op jit(solution)/shard_map/while/body/eval_jaxpr/ppermute | solution.py:13
  378.1 10.9 %collective-permute-done = f32[4,16384]{1,0:T(4,128)S(1)} collective-permute-done((f32[4,16384]{1,0:T(4,128)S(1)}, f32[4,16384]{1,0:T(4,128)S(1)}, u32[]{:S(2)}, u32[]{:S(2)}) %collective-permute-start) | collective-permute-done | bytes 262176 | tf_op jit(solution)/shard_map/while/body/eval_jaxpr/ppermute | solution.py:13
  392.3 10.9 %collective-permute-done = f32[4,16384]{1,0:T(4,128)S(1)} collective-permute-done((f32[4,16384]{1,0:T(4,128)S(1)}, f32[4,16384]{1,0:T(4,128)S(1)}, u32[]{:S(2)}, u32[]{:S(2)}) %collective-permute-start) | collective-permute-done | bytes 262176 | tf_op jit(solution)/shard_map/while/body/eval_jaxpr/ppermute | solution.py:13
  406.6 10.0 %collective-permute-done = f32[4,16384]{1,0:T(4,128)S(1)} collective-permute-done((f32[4,16384]{1,0:T(4,128)S(1)}, f32[4,16384]{1,0:T(4,128)S(1)}, u32[]{:S(2)}, u32[]{:S(2)}) %collective-permute-start) | collective-permute-done | bytes 262176 | tf_op jit(solution)/shard_map/while/body/eval_jaxpr/ppermute | solution.py:13
  419.9 9.2 %collective-permute-done = f32[4,16384]{1,0:T(4,128)S(1)} collective-permute-done((f32[4,16384]{1,0:T(4,128)S(1)}, f32[4,16384]{1,0:T(4,128)S(1)}, u32[]{:S(2)}, u32[]{:S(2)}) %collective-permute-start) | collective-permute-done | bytes 262176 | tf_op jit(solution)/shard_map/while/body/eval_jaxpr/ppermute | solution.py:13
  515.5 9.6 %collective-permute-done = f32[4,16384]{1,0:T(4,128)S(1)} collective-permute-done((f32[4,16384]{1,0:T(4,128)S(1)}, f32[4,16384]{1,0:T(4,128)S(1)}, u32[]{:S(2)}, u32[]{:S(2)}) %collective-permute-start) | collective-permute-done | bytes 262176 | tf_op jit(solution)/shard_map/while/body/eval_jaxpr/ppermute | solution.py:13
  528.5 10.8 %collective-permute-done = f32[4,16384]{1,0:T(4,128)S(1)} collective-permute-done((f32[4,16384]{1,0:T(4,128)S(1)}, f32[4,16384]{1,0:T(4,128)S(1)}, u32[]{:S(2)}, u32[]{:S(2)}) %collective-permute-start) | collective-permute-done | bytes 262176 | tf_op jit(solution)/shard_map/while/body/eval_jaxpr/ppermute | solution.py:13
  543.8 12.5 %scatter_fusion = f32[256,2,128]{2,1,0:T(2,128)} fusion(f32[256,2,128]{2,1,0:T(2,128)} %broadcast.154.clone, s32[128]{0:T(128)S(1)} %fusion.14, f32[128,2,128]{2,1,0:T(2,128)S(1)} %fusion.4), kind=kCustom, calls=%fused_computation.1 | custom fusion | bytes 393728 | tf_op jit(solution)/shard_map/scatter | solution.py:93
  556.2 43.4 %all-to-all-start.1 = ((f32[8,32,2,128]{3,2,1,0:T(2,128)}), f32[8,32,2,128]{3,2,1,0:T(2,128)S(1)}, u32[]{:S(2)}, u32[]{:S(2)}) async-start(f32[8,32,2,128]{3,2,1,0:T(2,128)} %bitcast.21), calls=%async_computation.1 | async-start | bytes 524288 | tf_op jit(solution)/shard_map/all_to_all | solution.py:95
  606.2 8.7 %scatter_fusion.1 = f32[256,2,128]{2,1,0:T(2,128)S(1)} fusion(f32[256,2,128]{2,1,0:T(2,128)S(1)} %broadcast.154, s32[256]{0:T(256)S(1)} %bitcast.85, f32[256,2,128]{2,1,0:T(2,128)S(1)} %bitcast.80), kind=kCustom, calls=%fused_computation.2 | custom fusion | flops 65536 | bytes 787456 | tf_op jit(solution)/shard_map/scatter-add | solution.py:104
  (209 shorter events, 247.9 us)
Async XLA Ops:
  6.5 142.5 %all-reduce.4.cloned.1.call-start = ((), (), s32[]{:S(2)}) async-start(), calls=%async_computation.2 | async-start | bytes 262144 | tf_op jit(solution)/shard_map/psum | solution.py:56
  12.4 543.8 %all-to-all-start = ((s32[8,1,32]{2,1,0:T(1,128)}), s32[8,1,32]{2,1,0:T(1,128)S(1)}, u32[]{:S(2)}, u32[]{:S(2)}) async-start(s32[8,1,32]{2,1,0:T(1,128)} %all_to_all.9), calls=%async_computation | async-start | bytes 8192 | tf_op jit(solution)/shard_map/all_to_all | solution.py:98
  153.0 10.4 %collective-permute-start = (f32[4,16384]{1,0:T(4,128)S(1)}, f32[4,16384]{1,0:T(4,128)S(1)}, u32[]{:S(2)}, u32[]{:S(2)}) collective-permute-start(f32[4,16384]{1,0:T(4,128)S(1)} %pad_maximum_fusion.7), channel_id=1, source_target_pairs={{8,0},{16,8},{24,16},{32,24},{40,32},{48,40},{56,48},{64,56},{72,6... | collective-permute-start | bytes 786440 | tf_op jit(solution)/shard_map/while/body/eval_jaxpr/ppermute | solution.py:13
  164.9 10.4 %collective-permute-start = (f32[4,16384]{1,0:T(4,128)S(1)}, f32[4,16384]{1,0:T(4,128)S(1)}, u32[]{:S(2)}, u32[]{:S(2)}) collective-permute-start(f32[4,16384]{1,0:T(4,128)S(1)} %pad_maximum_fusion.7), channel_id=1, source_target_pairs={{8,0},{16,8},{24,16},{32,24},{40,32},{48,40},{56,48},{64,56},{72,6... | collective-permute-start | bytes 786440 | tf_op jit(solution)/shard_map/while/body/eval_jaxpr/ppermute | solution.py:13
  176.7 10.4 %collective-permute-start = (f32[4,16384]{1,0:T(4,128)S(1)}, f32[4,16384]{1,0:T(4,128)S(1)}, u32[]{:S(2)}, u32[]{:S(2)}) collective-permute-start(f32[4,16384]{1,0:T(4,128)S(1)} %pad_maximum_fusion.7), channel_id=1, source_target_pairs={{8,0},{16,8},{24,16},{32,24},{40,32},{48,40},{56,48},{64,56},{72,6... | collective-permute-start | bytes 786440 | tf_op jit(solution)/shard_map/while/body/eval_jaxpr/ppermute | solution.py:13
  200.5 10.6 %collective-permute-start = (f32[4,16384]{1,0:T(4,128)S(1)}, f32[4,16384]{1,0:T(4,128)S(1)}, u32[]{:S(2)}, u32[]{:S(2)}) collective-permute-start(f32[4,16384]{1,0:T(4,128)S(1)} %pad_maximum_fusion.7), channel_id=1, source_target_pairs={{8,0},{16,8},{24,16},{32,24},{40,32},{48,40},{56,48},{64,56},{72,6... | collective-permute-start | bytes 786440 | tf_op jit(solution)/shard_map/while/body/eval_jaxpr/ppermute | solution.py:13
  212.5 11.8 %collective-permute-start = (f32[4,16384]{1,0:T(4,128)S(1)}, f32[4,16384]{1,0:T(4,128)S(1)}, u32[]{:S(2)}, u32[]{:S(2)}) collective-permute-start(f32[4,16384]{1,0:T(4,128)S(1)} %pad_maximum_fusion.7), channel_id=1, source_target_pairs={{8,0},{16,8},{24,16},{32,24},{40,32},{48,40},{56,48},{64,56},{72,6... | collective-permute-start | bytes 786440 | tf_op jit(solution)/shard_map/while/body/eval_jaxpr/ppermute | solution.py:13
  225.7 12.9 %collective-permute-start = (f32[4,16384]{1,0:T(4,128)S(1)}, f32[4,16384]{1,0:T(4,128)S(1)}, u32[]{:S(2)}, u32[]{:S(2)}) collective-permute-start(f32[4,16384]{1,0:T(4,128)S(1)} %pad_maximum_fusion.7), channel_id=1, source_target_pairs={{8,0},{16,8},{24,16},{32,24},{40,32},{48,40},{56,48},{64,56},{72,6... | collective-permute-start | bytes 786440 | tf_op jit(solution)/shard_map/while/body/eval_jaxpr/ppermute | solution.py:13
  240.1 12.7 %collective-permute-start = (f32[4,16384]{1,0:T(4,128)S(1)}, f32[4,16384]{1,0:T(4,128)S(1)}, u32[]{:S(2)}, u32[]{:S(2)}) collective-permute-start(f32[4,16384]{1,0:T(4,128)S(1)} %pad_maximum_fusion.7), channel_id=1, source_target_pairs={{8,0},{16,8},{24,16},{32,24},{40,32},{48,40},{56,48},{64,56},{72,6... | collective-permute-start | bytes 786440 | tf_op jit(solution)/shard_map/while/body/eval_jaxpr/ppermute | solution.py:13
  254.2 11.9 %collective-permute-start = (f32[4,16384]{1,0:T(4,128)S(1)}, f32[4,16384]{1,0:T(4,128)S(1)}, u32[]{:S(2)}, u32[]{:S(2)}) collective-permute-start(f32[4,16384]{1,0:T(4,128)S(1)} %pad_maximum_fusion.7), channel_id=1, source_target_pairs={{8,0},{16,8},{24,16},{32,24},{40,32},{48,40},{56,48},{64,56},{72,6... | collective-permute-start | bytes 786440 | tf_op jit(solution)/shard_map/while/body/eval_jaxpr/ppermute | solution.py:13
  267.5 11.0 %collective-permute-start = (f32[4,16384]{1,0:T(4,128)S(1)}, f32[4,16384]{1,0:T(4,128)S(1)}, u32[]{:S(2)}, u32[]{:S(2)}) collective-permute-start(f32[4,16384]{1,0:T(4,128)S(1)} %pad_maximum_fusion.7), channel_id=1, source_target_pairs={{8,0},{16,8},{24,16},{32,24},{40,32},{48,40},{56,48},{64,56},{72,6... | collective-permute-start | bytes 786440 | tf_op jit(solution)/shard_map/while/body/eval_jaxpr/ppermute | solution.py:13
  279.9 10.4 %collective-permute-start = (f32[4,16384]{1,0:T(4,128)S(1)}, f32[4,16384]{1,0:T(4,128)S(1)}, u32[]{:S(2)}, u32[]{:S(2)}) collective-permute-start(f32[4,16384]{1,0:T(4,128)S(1)} %pad_maximum_fusion.7), channel_id=1, source_target_pairs={{8,0},{16,8},{24,16},{32,24},{40,32},{48,40},{56,48},{64,56},{72,6... | collective-permute-start | bytes 786440 | tf_op jit(solution)/shard_map/while/body/eval_jaxpr/ppermute | solution.py:13
  291.8 10.4 %collective-permute-start = (f32[4,16384]{1,0:T(4,128)S(1)}, f32[4,16384]{1,0:T(4,128)S(1)}, u32[]{:S(2)}, u32[]{:S(2)}) collective-permute-start(f32[4,16384]{1,0:T(4,128)S(1)} %pad_maximum_fusion.7), channel_id=1, source_target_pairs={{8,0},{16,8},{24,16},{32,24},{40,32},{48,40},{56,48},{64,56},{72,6... | collective-permute-start | bytes 786440 | tf_op jit(solution)/shard_map/while/body/eval_jaxpr/ppermute | solution.py:13
  315.5 10.4 %collective-permute-start = (f32[4,16384]{1,0:T(4,128)S(1)}, f32[4,16384]{1,0:T(4,128)S(1)}, u32[]{:S(2)}, u32[]{:S(2)}) collective-permute-start(f32[4,16384]{1,0:T(4,128)S(1)} %pad_maximum_fusion.7), channel_id=1, source_target_pairs={{8,0},{16,8},{24,16},{32,24},{40,32},{48,40},{56,48},{64,56},{72,6... | collective-permute-start | bytes 786440 | tf_op jit(solution)/shard_map/while/body/eval_jaxpr/ppermute | solution.py:13
  327.4 10.4 %collective-permute-start = (f32[4,16384]{1,0:T(4,128)S(1)}, f32[4,16384]{1,0:T(4,128)S(1)}, u32[]{:S(2)}, u32[]{:S(2)}) collective-permute-start(f32[4,16384]{1,0:T(4,128)S(1)} %pad_maximum_fusion.7), channel_id=1, source_target_pairs={{8,0},{16,8},{24,16},{32,24},{40,32},{48,40},{56,48},{64,56},{72,6... | collective-permute-start | bytes 786440 | tf_op jit(solution)/shard_map/while/body/eval_jaxpr/ppermute | solution.py:13
  351.1 10.5 %collective-permute-start = (f32[4,16384]{1,0:T(4,128)S(1)}, f32[4,16384]{1,0:T(4,128)S(1)}, u32[]{:S(2)}, u32[]{:S(2)}) collective-permute-start(f32[4,16384]{1,0:T(4,128)S(1)} %pad_maximum_fusion.7), channel_id=1, source_target_pairs={{8,0},{16,8},{24,16},{32,24},{40,32},{48,40},{56,48},{64,56},{72,6... | collective-permute-start | bytes 786440 | tf_op jit(solution)/shard_map/while/body/eval_jaxpr/ppermute | solution.py:13
  363.0 11.7 %collective-permute-start = (f32[4,16384]{1,0:T(4,128)S(1)}, f32[4,16384]{1,0:T(4,128)S(1)}, u32[]{:S(2)}, u32[]{:S(2)}) collective-permute-start(f32[4,16384]{1,0:T(4,128)S(1)} %pad_maximum_fusion.7), channel_id=1, source_target_pairs={{8,0},{16,8},{24,16},{32,24},{40,32},{48,40},{56,48},{64,56},{72,6... | collective-permute-start | bytes 786440 | tf_op jit(solution)/shard_map/while/body/eval_jaxpr/ppermute | solution.py:13
  376.1 12.8 %collective-permute-start = (f32[4,16384]{1,0:T(4,128)S(1)}, f32[4,16384]{1,0:T(4,128)S(1)}, u32[]{:S(2)}, u32[]{:S(2)}) collective-permute-start(f32[4,16384]{1,0:T(4,128)S(1)} %pad_maximum_fusion.7), channel_id=1, source_target_pairs={{8,0},{16,8},{24,16},{32,24},{40,32},{48,40},{56,48},{64,56},{72,6... | collective-permute-start | bytes 786440 | tf_op jit(solution)/shard_map/while/body/eval_jaxpr/ppermute | solution.py:13
  390.4 12.8 %collective-permute-start = (f32[4,16384]{1,0:T(4,128)S(1)}, f32[4,16384]{1,0:T(4,128)S(1)}, u32[]{:S(2)}, u32[]{:S(2)}) collective-permute-start(f32[4,16384]{1,0:T(4,128)S(1)} %pad_maximum_fusion.7), channel_id=1, source_target_pairs={{8,0},{16,8},{24,16},{32,24},{40,32},{48,40},{56,48},{64,56},{72,6... | collective-permute-start | bytes 786440 | tf_op jit(solution)/shard_map/while/body/eval_jaxpr/ppermute | solution.py:13
  404.6 12.0 %collective-permute-start = (f32[4,16384]{1,0:T(4,128)S(1)}, f32[4,16384]{1,0:T(4,128)S(1)}, u32[]{:S(2)}, u32[]{:S(2)}) collective-permute-start(f32[4,16384]{1,0:T(4,128)S(1)} %pad_maximum_fusion.7), channel_id=1, source_target_pairs={{8,0},{16,8},{24,16},{32,24},{40,32},{48,40},{56,48},{64,56},{72,6... | collective-permute-start | bytes 786440 | tf_op jit(solution)/shard_map/while/body/eval_jaxpr/ppermute | solution.py:13
  418.0 11.1 %collective-permute-start = (f32[4,16384]{1,0:T(4,128)S(1)}, f32[4,16384]{1,0:T(4,128)S(1)}, u32[]{:S(2)}, u32[]{:S(2)}) collective-permute-start(f32[4,16384]{1,0:T(4,128)S(1)} %pad_maximum_fusion.7), channel_id=1, source_target_pairs={{8,0},{16,8},{24,16},{32,24},{40,32},{48,40},{56,48},{64,56},{72,6... | collective-permute-start | bytes 786440 | tf_op jit(solution)/shard_map/while/body/eval_jaxpr/ppermute | solution.py:13
  513.6 11.6 %collective-permute-start = (f32[4,16384]{1,0:T(4,128)S(1)}, f32[4,16384]{1,0:T(4,128)S(1)}, u32[]{:S(2)}, u32[]{:S(2)}) collective-permute-start(f32[4,16384]{1,0:T(4,128)S(1)} %pad_maximum_fusion.7), channel_id=1, source_target_pairs={{8,0},{16,8},{24,16},{32,24},{40,32},{48,40},{56,48},{64,56},{72,6... | collective-permute-start | bytes 786440 | tf_op jit(solution)/shard_map/while/body/eval_jaxpr/ppermute | solution.py:13
  526.6 12.7 %collective-permute-start = (f32[4,16384]{1,0:T(4,128)S(1)}, f32[4,16384]{1,0:T(4,128)S(1)}, u32[]{:S(2)}, u32[]{:S(2)}) collective-permute-start(f32[4,16384]{1,0:T(4,128)S(1)} %pad_maximum_fusion.7), channel_id=1, source_target_pairs={{8,0},{16,8},{24,16},{32,24},{40,32},{48,40},{56,48},{64,56},{72,6... | collective-permute-start | bytes 786440 | tf_op jit(solution)/shard_map/while/body/eval_jaxpr/ppermute | solution.py:13
  556.2 49.9 %all-to-all-start.1 = ((f32[8,32,2,128]{3,2,1,0:T(2,128)}), f32[8,32,2,128]{3,2,1,0:T(2,128)S(1)}, u32[]{:S(2)}, u32[]{:S(2)}) async-start(f32[8,32,2,128]{3,2,1,0:T(2,128)} %bitcast.21), calls=%async_computation.1 | async-start | bytes 524288 | tf_op jit(solution)/shard_map/all_to_all | solution.py:95
  (14 other events, 125.2 us)
Sparse Core Ops, SparseCore 0:
  10.8 138.2 all-reduce.3
where the time goes:
time: 642 us; the launch traced here: 640 us
  waiting for transfers between devices  425 us (66%)
  starting transfers between devices  119 us (19%)
  other arithmetic  60.1 us (9%)
  local copies, waits for them, and re-layouts  17.1 us (3%)
  between operations  14.9 us (2%)
    ppermute x31, waiting for transfers between devices, from_behind(): lax.ppermute(value, axis, [(source, source + steps) for source in range(l...  283 us
    psum x1, waiting for transfers between devices, per_device(): shear = lax.psum(local_terms, 'depth')  130 us
    ppermute x31, starting transfers between devices, from_behind(): lax.ppermute(value, axis, [(source, source + steps) for source in range(l...  60.4 us
    all_to_all x1, starting transfers between devices, per_device(): lax.all_to_all(send_data.reshape(n_tile, slots, 2, width), 'tile', split_...  43.4 us
    sub x31, other arithmetic, sweep(): new_one = xb_one - (jxx[0] * tp_one + jxy[0] * tp_two)  27.6 us
  transfers between devices with their start and end apart: 38, of which 35 were waited for; matrix products, arithmetic and copies ran while one was open for 11% of the time, Pallas kernels for 0%

commit v1 on v0

--- a/solution.py
+++ b/solution.py
@@ -53,7 +53,9 @@
             -jnp.sum(plane_weight[:, None] * jxy, axis=0),
         ]
     )
-    shear = lax.psum(local_terms, "depth")
+    shear = local_terms
+    for hop in (1, 2, 4, 8, 16):
+        shear = shear + lax.ppermute(shear, "depth", [(dev, dev ^ hop) for dev in range(32)])
     cross = -shear[0] * jnp.sin(2.0 * ray_angle) + shear[1] * jnp.cos(2.0 * ray_angle)
     seed_state = jnp.stack(
         [

time: 642 us -> 516 us (0.80)
  waiting for transfers between devices: 425 us -> 309 us
  between operations: 14.9 us -> 1.53 us
    psum x1 -> x0, waiting for transfers between devices: 130 us -> none  [per_device(): shear = lax.psum(local_terms, 'depth')]
    ppermute x0 -> x5, waiting for transfers between devices: none -> 13 us  [per_device(): lax.ppermute(shear, 'depth', [(dev, dev ^ hop) for dev in range(32)])]
    ppermute x0 -> x5, starting transfers between devices: none -> 7.88 us  [per_device(): lax.ppermute(shear, 'depth', [(dev, dev ^ hop) for dev in range(32)])]
  transfers between devices with their start and end apart: 38 -> 42, of which waited for: 35 -> 38; matrix products, arithmetic and copies ran while one was open for 11% -> 13% of each run, Pallas kernels for 0% -> 0%
where the time goes in v1:
time: 516 us; the launch traced here: 514 us
  waiting for transfers between devices  309 us (60%)
  starting transfers between devices  123 us (24%)
  other arithmetic  59 us (11%)
  local copies, waits for them, and re-layouts  17.1 us (3%)
    ppermute x31, waiting for transfers between devices, from_behind(): lax.ppermute(value, axis, [(source, source + steps) for source in range(l...  284 us
    ppermute x31, starting transfers between devices, from_behind(): lax.ppermute(value, axis, [(source, source + steps) for source in range(l...  60.1 us
    all_to_all x1, starting transfers between devices, per_device(): lax.all_to_all(send_data.reshape(n_tile, slots, 2, width), 'tile', split_...  37.3 us
    sub x31, other arithmetic, sweep(): new_one = xb_one - (jxx[0] * tp_one + jxy[0] * tp_two)  27.6 us
    ppermute x5, waiting for transfers between devices, per_device(): lax.ppermute(shear, 'depth', [(dev, dev ^ hop) for dev in range(32)])  13 us
    scatter x1, local copies, waits for them, and re-layouts, per_device(): jnp.zeros((n_tile * slots, 2, width), jnp.float32).at[slot].set(contrib[0])  12.5 us
  transfers between devices with their start and end apart: 42, of which 38 were waited for; matrix products, arithmetic and copies ran while one was open for 13% of the time, Pallas kernels for 0%

profile of v1, /device:TPU:103, one launch (start us, length us, event | category | flops | bytes accessed | tf_op | source)
XLA Modules:
  0.0 514.2 jit_solution(17493445885441464760)
XLA Ops:
  38.2 388.0 %while.10 = (s32[]{:T(128)}, f32[4,16384]{1,0:T(4,128)S(1)}, pred[]{:T(512)}, f32[1,1,16384]{2,1,0:T(1,128)S(1)}, f32[1]{0:T(128)}, /*index=5*/f32[1,1,16384]{2,...) while((s32[]{:T(128)}, f32[4,16384]{1,0:T(4,128)S(1)}, pred[]{:T(512)}, ...), condition=%wide.region_3.4_spmd, body=%wide.region_2.3_spmd.sunk | while | flops 458754 | bytes 3342474 | solution.py:86
  42.0 9.8 %collective-permute-done = f32[4,16384]{1,0:T(4,128)S(1)} collective-permute-done((f32[4,16384]{1,0:T(4,128)S(1)}, f32[4,16384]{1,0:T(4,128)S(1)}, u32[]{:S(2)}, u32[]{:S(2)}) %collective-permute-start) | collective-permute-done | bytes 262176 | tf_op jit(solution)/shard_map/while/body/eval_jaxpr/ppermute | solution.py:13
  55.1 9.5 %collective-permute-done = f32[4,16384]{1,0:T(4,128)S(1)} collective-permute-done((f32[4,16384]{1,0:T(4,128)S(1)}, f32[4,16384]{1,0:T(4,128)S(1)}, u32[]{:S(2)}, u32[]{:S(2)}) %collective-permute-start) | collective-permute-done | bytes 262176 | tf_op jit(solution)/shard_map/while/body/eval_jaxpr/ppermute | solution.py:13
  67.9 8.5 %collective-permute-done = f32[4,16384]{1,0:T(4,128)S(1)} collective-permute-done((f32[4,16384]{1,0:T(4,128)S(1)}, f32[4,16384]{1,0:T(4,128)S(1)}, u32[]{:S(2)}, u32[]{:S(2)}) %collective-permute-start) | collective-permute-done | bytes 262176 | tf_op jit(solution)/shard_map/while/body/eval_jaxpr/ppermute | solution.py:13
  79.8 8.5 %collective-permute-done = f32[4,16384]{1,0:T(4,128)S(1)} collective-permute-done((f32[4,16384]{1,0:T(4,128)S(1)}, f32[4,16384]{1,0:T(4,128)S(1)}, u32[]{:S(2)}, u32[]{:S(2)}) %collective-permute-start) | collective-permute-done | bytes 262176 | tf_op jit(solution)/shard_map/while/body/eval_jaxpr/ppermute | solution.py:13
  91.6 8.5 %collective-permute-done = f32[4,16384]{1,0:T(4,128)S(1)} collective-permute-done((f32[4,16384]{1,0:T(4,128)S(1)}, f32[4,16384]{1,0:T(4,128)S(1)}, u32[]{:S(2)}, u32[]{:S(2)}) %collective-permute-start) | collective-permute-done | bytes 262176 | tf_op jit(solution)/shard_map/while/body/eval_jaxpr/ppermute | solution.py:13
  115.4 8.5 %collective-permute-done = f32[4,16384]{1,0:T(4,128)S(1)} collective-permute-done((f32[4,16384]{1,0:T(4,128)S(1)}, f32[4,16384]{1,0:T(4,128)S(1)}, u32[]{:S(2)}, u32[]{:S(2)}) %collective-permute-start) | collective-permute-done | bytes 262176 | tf_op jit(solution)/shard_map/while/body/eval_jaxpr/ppermute | solution.py:13
  127.2 8.5 %collective-permute-done = f32[4,16384]{1,0:T(4,128)S(1)} collective-permute-done((f32[4,16384]{1,0:T(4,128)S(1)}, f32[4,16384]{1,0:T(4,128)S(1)}, u32[]{:S(2)}, u32[]{:S(2)}) %collective-permute-start) | collective-permute-done | bytes 262176 | tf_op jit(solution)/shard_map/while/body/eval_jaxpr/ppermute | solution.py:13
  150.9 9.4 %collective-permute-done = f32[4,16384]{1,0:T(4,128)S(1)} collective-permute-done((f32[4,16384]{1,0:T(4,128)S(1)}, f32[4,16384]{1,0:T(4,128)S(1)}, u32[]{:S(2)}, u32[]{:S(2)}) %collective-permute-start) | collective-permute-done | bytes 262176 | tf_op jit(solution)/shard_map/while/body/eval_jaxpr/ppermute | solution.py:13
  163.7 10.5 %collective-permute-done = f32[4,16384]{1,0:T(4,128)S(1)} collective-permute-done((f32[4,16384]{1,0:T(4,128)S(1)}, f32[4,16384]{1,0:T(4,128)S(1)}, u32[]{:S(2)}, u32[]{:S(2)}) %collective-permute-start) | collective-permute-done | bytes 262176 | tf_op jit(solution)/shard_map/while/body/eval_jaxpr/ppermute | solution.py:13
  177.5 11.3 %collective-permute-done = f32[4,16384]{1,0:T(4,128)S(1)} collective-permute-done((f32[4,16384]{1,0:T(4,128)S(1)}, f32[4,16384]{1,0:T(4,128)S(1)}, u32[]{:S(2)}, u32[]{:S(2)}) %collective-permute-start) | collective-permute-done | bytes 262176 | tf_op jit(solution)/shard_map/while/body/eval_jaxpr/ppermute | solution.py:13
  192.1 10.4 %collective-permute-done = f32[4,16384]{1,0:T(4,128)S(1)} collective-permute-done((f32[4,16384]{1,0:T(4,128)S(1)}, f32[4,16384]{1,0:T(4,128)S(1)}, u32[]{:S(2)}, u32[]{:S(2)}) %collective-permute-start) | collective-permute-done | bytes 262176 | tf_op jit(solution)/shard_map/while/body/eval_jaxpr/ppermute | solution.py:13
  205.9 9.6 %collective-permute-done = f32[4,16384]{1,0:T(4,128)S(1)} collective-permute-done((f32[4,16384]{1,0:T(4,128)S(1)}, f32[4,16384]{1,0:T(4,128)S(1)}, u32[]{:S(2)}, u32[]{:S(2)}) %collective-permute-start) | collective-permute-done | bytes 262176 | tf_op jit(solution)/shard_map/while/body/eval_jaxpr/ppermute | solution.py:13
  230.7 8.5 %collective-permute-done = f32[4,16384]{1,0:T(4,128)S(1)} collective-permute-done((f32[4,16384]{1,0:T(4,128)S(1)}, f32[4,16384]{1,0:T(4,128)S(1)}, u32[]{:S(2)}, u32[]{:S(2)}) %collective-permute-start) | collective-permute-done | bytes 262176 | tf_op jit(solution)/shard_map/while/body/eval_jaxpr/ppermute | solution.py:13
  242.5 8.5 %collective-permute-done = f32[4,16384]{1,0:T(4,128)S(1)} collective-permute-done((f32[4,16384]{1,0:T(4,128)S(1)}, f32[4,16384]{1,0:T(4,128)S(1)}, u32[]{:S(2)}, u32[]{:S(2)}) %collective-permute-start) | collective-permute-done | bytes 262176 | tf_op jit(solution)/shard_map/while/body/eval_jaxpr/ppermute | solution.py:13
  301.8 9.3 %collective-permute-done = f32[4,16384]{1,0:T(4,128)S(1)} collective-permute-done((f32[4,16384]{1,0:T(4,128)S(1)}, f32[4,16384]{1,0:T(4,128)S(1)}, u32[]{:S(2)}, u32[]{:S(2)}) %collective-permute-start) | collective-permute-done | bytes 262176 | tf_op jit(solution)/shard_map/while/body/eval_jaxpr/ppermute | solution.py:13
  314.5 10.4 %collective-permute-done = f32[4,16384]{1,0:T(4,128)S(1)} collective-permute-done((f32[4,16384]{1,0:T(4,128)S(1)}, f32[4,16384]{1,0:T(4,128)S(1)}, u32[]{:S(2)}, u32[]{:S(2)}) %collective-permute-start) | collective-permute-done | bytes 262176 | tf_op jit(solution)/shard_map/while/body/eval_jaxpr/ppermute | solution.py:13
  328.2 11.4 %collective-permute-done = f32[4,16384]{1,0:T(4,128)S(1)} collective-permute-done((f32[4,16384]{1,0:T(4,128)S(1)}, f32[4,16384]{1,0:T(4,128)S(1)}, u32[]{:S(2)}, u32[]{:S(2)}) %collective-permute-start) | collective-permute-done | bytes 262176 | tf_op jit(solution)/shard_map/while/body/eval_jaxpr/ppermute | solution.py:13
  342.9 10.5 %collective-permute-done = f32[4,16384]{1,0:T(4,128)S(1)} collective-permute-done((f32[4,16384]{1,0:T(4,128)S(1)}, f32[4,16384]{1,0:T(4,128)S(1)}, u32[]{:S(2)}, u32[]{:S(2)}) %collective-permute-start) | collective-permute-done | bytes 262176 | tf_op jit(solution)/shard_map/while/body/eval_jaxpr/ppermute | solution.py:13
  356.8 9.7 %collective-permute-done = f32[4,16384]{1,0:T(4,128)S(1)} collective-permute-done((f32[4,16384]{1,0:T(4,128)S(1)}, f32[4,16384]{1,0:T(4,128)S(1)}, u32[]{:S(2)}, u32[]{:S(2)}) %collective-permute-start) | collective-permute-done | bytes 262176 | tf_op jit(solution)/shard_map/while/body/eval_jaxpr/ppermute | solution.py:13
  369.8 8.8 %collective-permute-done = f32[4,16384]{1,0:T(4,128)S(1)} collective-permute-done((f32[4,16384]{1,0:T(4,128)S(1)}, f32[4,16384]{1,0:T(4,128)S(1)}, u32[]{:S(2)}, u32[]{:S(2)}) %collective-permute-start) | collective-permute-done | bytes 262176 | tf_op jit(solution)/shard_map/while/body/eval_jaxpr/ppermute | solution.py:13
  430.6 12.5 %scatter_fusion = f32[256,2,128]{2,1,0:T(2,128)} fusion(f32[256,2,128]{2,1,0:T(2,128)} %broadcast.154.clone, s32[128]{0:T(128)S(1)} %fusion.14, f32[128,2,128]{2,1,0:T(2,128)S(1)} %fusion.4), kind=kCustom, calls=%fused_computation.1 | custom fusion | bytes 393728 | tf_op jit(solution)/shard_map/scatter | solution.py:95
  443.1 37.3 %all-to-all-start.1 = ((f32[8,32,2,128]{3,2,1,0:T(2,128)}), f32[8,32,2,128]{3,2,1,0:T(2,128)S(1)}, u32[]{:S(2)}, u32[]{:S(2)}) async-start(f32[8,32,2,128]{3,2,1,0:T(2,128)} %bitcast.21), calls=%async_computation.1 | async-start | bytes 524288 | tf_op jit(solution)/shard_map/all_to_all | solution.py:97
  486.9 8.7 %scatter_fusion.1 = f32[256,2,128]{2,1,0:T(2,128)S(1)} fusion(f32[256,2,128]{2,1,0:T(2,128)S(1)} %broadcast.154, s32[256]{0:T(256)S(1)} %bitcast.85, f32[256,2,128]{2,1,0:T(2,128)S(1)} %bitcast.80), kind=kCustom, calls=%fused_computation.2 | custom fusion | flops 65536 | bytes 787456 | tf_op jit(solution)/shard_map/scatter-add | solution.py:106
  (221 shorter events, 262.8 us)
Async XLA Ops:
  16.0 10.9 %collective-permute-start.4 = (f32[2,16384]{1,0:T(2,128)S(1)}, f32[2,16384]{1,0:T(2,128)S(1)}, u32[]{:S(2)}, u32[]{:S(2)}) collective-permute-start(f32[2,16384]{1,0:T(2,128)S(1)} %add.113), channel_id=1, source_target_pairs={{0,64},{8,72},{16,80},{24,88},{32,96},{40,104},{48,112},{56,120},{... | collective-permute-start | bytes 393224 | tf_op jit(solution)/shard_map/ppermute | solution.py:58
  18.6 424.5 %all-to-all-start = ((s32[8,1,32]{2,1,0:T(1,128)}), s32[8,1,32]{2,1,0:T(1,128)S(1)}, u32[]{:S(2)}, u32[]{:S(2)}) async-start(s32[8,1,32]{2,1,0:T(1,128)} %all_to_all.9), calls=%async_computation | async-start | bytes 8192 | tf_op jit(solution)/shard_map/all_to_all | solution.py:100
  39.5 12.2 %collective-permute-start = (f32[4,16384]{1,0:T(4,128)S(1)}, f32[4,16384]{1,0:T(4,128)S(1)}, u32[]{:S(2)}, u32[]{:S(2)}) collective-permute-start(f32[4,16384]{1,0:T(4,128)S(1)} %pad_maximum_fusion.7), channel_id=1, source_target_pairs={{8,0},{16,8},{24,16},{32,24},{40,32},{48,40},{56,48},{64,56},{72,6... | collective-permute-start | bytes 786440 | tf_op jit(solution)/shard_map/while/body/eval_jaxpr/ppermute | solution.py:13
  53.2 11.4 %collective-permute-start = (f32[4,16384]{1,0:T(4,128)S(1)}, f32[4,16384]{1,0:T(4,128)S(1)}, u32[]{:S(2)}, u32[]{:S(2)}) collective-permute-start(f32[4,16384]{1,0:T(4,128)S(1)} %pad_maximum_fusion.7), channel_id=1, source_target_pairs={{8,0},{16,8},{24,16},{32,24},{40,32},{48,40},{56,48},{64,56},{72,6... | collective-permute-start | bytes 786440 | tf_op jit(solution)/shard_map/while/body/eval_jaxpr/ppermute | solution.py:13
  66.0 10.4 %collective-permute-start = (f32[4,16384]{1,0:T(4,128)S(1)}, f32[4,16384]{1,0:T(4,128)S(1)}, u32[]{:S(2)}, u32[]{:S(2)}) collective-permute-start(f32[4,16384]{1,0:T(4,128)S(1)} %pad_maximum_fusion.7), channel_id=1, source_target_pairs={{8,0},{16,8},{24,16},{32,24},{40,32},{48,40},{56,48},{64,56},{72,6... | collective-permute-start | bytes 786440 | tf_op jit(solution)/shard_map/while/body/eval_jaxpr/ppermute | solution.py:13
  77.8 10.4 %collective-permute-start = (f32[4,16384]{1,0:T(4,128)S(1)}, f32[4,16384]{1,0:T(4,128)S(1)}, u32[]{:S(2)}, u32[]{:S(2)}) collective-permute-start(f32[4,16384]{1,0:T(4,128)S(1)} %pad_maximum_fusion.7), channel_id=1, source_target_pairs={{8,0},{16,8},{24,16},{32,24},{40,32},{48,40},{56,48},{64,56},{72,6... | collective-permute-start | bytes 786440 | tf_op jit(solution)/shard_map/while/body/eval_jaxpr/ppermute | solution.py:13
  89.7 10.4 %collective-permute-start = (f32[4,16384]{1,0:T(4,128)S(1)}, f32[4,16384]{1,0:T(4,128)S(1)}, u32[]{:S(2)}, u32[]{:S(2)}) collective-permute-start(f32[4,16384]{1,0:T(4,128)S(1)} %pad_maximum_fusion.7), channel_id=1, source_target_pairs={{8,0},{16,8},{24,16},{32,24},{40,32},{48,40},{56,48},{64,56},{72,6... | collective-permute-start | bytes 786440 | tf_op jit(solution)/shard_map/while/body/eval_jaxpr/ppermute | solution.py:13
  113.4 10.4 %collective-permute-start = (f32[4,16384]{1,0:T(4,128)S(1)}, f32[4,16384]{1,0:T(4,128)S(1)}, u32[]{:S(2)}, u32[]{:S(2)}) collective-permute-start(f32[4,16384]{1,0:T(4,128)S(1)} %pad_maximum_fusion.7), channel_id=1, source_target_pairs={{8,0},{16,8},{24,16},{32,24},{40,32},{48,40},{56,48},{64,56},{72,6... | collective-permute-start | bytes 786440 | tf_op jit(solution)/shard_map/while/body/eval_jaxpr/ppermute | solution.py:13
  125.3 10.4 %collective-permute-start = (f32[4,16384]{1,0:T(4,128)S(1)}, f32[4,16384]{1,0:T(4,128)S(1)}, u32[]{:S(2)}, u32[]{:S(2)}) collective-permute-start(f32[4,16384]{1,0:T(4,128)S(1)} %pad_maximum_fusion.7), channel_id=1, source_target_pairs={{8,0},{16,8},{24,16},{32,24},{40,32},{48,40},{56,48},{64,56},{72,6... | collective-permute-start | bytes 786440 | tf_op jit(solution)/shard_map/while/body/eval_jaxpr/ppermute | solution.py:13
  149.0 11.3 %collective-permute-start = (f32[4,16384]{1,0:T(4,128)S(1)}, f32[4,16384]{1,0:T(4,128)S(1)}, u32[]{:S(2)}, u32[]{:S(2)}) collective-permute-start(f32[4,16384]{1,0:T(4,128)S(1)} %pad_maximum_fusion.7), channel_id=1, source_target_pairs={{8,0},{16,8},{24,16},{32,24},{40,32},{48,40},{56,48},{64,56},{72,6... | collective-permute-start | bytes 786440 | tf_op jit(solution)/shard_map/while/body/eval_jaxpr/ppermute | solution.py:13
  161.7 12.4 %collective-permute-start = (f32[4,16384]{1,0:T(4,128)S(1)}, f32[4,16384]{1,0:T(4,128)S(1)}, u32[]{:S(2)}, u32[]{:S(2)}) collective-permute-start(f32[4,16384]{1,0:T(4,128)S(1)} %pad_maximum_fusion.7), channel_id=1, source_target_pairs={{8,0},{16,8},{24,16},{32,24},{40,32},{48,40},{56,48},{64,56},{72,6... | collective-permute-start | bytes 786440 | tf_op jit(solution)/shard_map/while/body/eval_jaxpr/ppermute | solution.py:13
  175.6 13.2 %collective-permute-start = (f32[4,16384]{1,0:T(4,128)S(1)}, f32[4,16384]{1,0:T(4,128)S(1)}, u32[]{:S(2)}, u32[]{:S(2)}) collective-permute-start(f32[4,16384]{1,0:T(4,128)S(1)} %pad_maximum_fusion.7), channel_id=1, source_target_pairs={{8,0},{16,8},{24,16},{32,24},{40,32},{48,40},{56,48},{64,56},{72,6... | collective-permute-start | bytes 786440 | tf_op jit(solution)/shard_map/while/body/eval_jaxpr/ppermute | solution.py:13
  190.2 12.3 %collective-permute-start = (f32[4,16384]{1,0:T(4,128)S(1)}, f32[4,16384]{1,0:T(4,128)S(1)}, u32[]{:S(2)}, u32[]{:S(2)}) collective-permute-start(f32[4,16384]{1,0:T(4,128)S(1)} %pad_maximum_fusion.7), channel_id=1, source_target_pairs={{8,0},{16,8},{24,16},{32,24},{40,32},{48,40},{56,48},{64,56},{72,6... | collective-permute-start | bytes 786440 | tf_op jit(solution)/shard_map/while/body/eval_jaxpr/ppermute | solution.py:13
  204.0 11.5 %collective-permute-start = (f32[4,16384]{1,0:T(4,128)S(1)}, f32[4,16384]{1,0:T(4,128)S(1)}, u32[]{:S(2)}, u32[]{:S(2)}) collective-permute-start(f32[4,16384]{1,0:T(4,128)S(1)} %pad_maximum_fusion.7), channel_id=1, source_target_pairs={{8,0},{16,8},{24,16},{32,24},{40,32},{48,40},{56,48},{64,56},{72,6... | collective-permute-start | bytes 786440 | tf_op jit(solution)/shard_map/while/body/eval_jaxpr/ppermute | solution.py:13
  228.8 10.4 %collective-permute-start = (f32[4,16384]{1,0:T(4,128)S(1)}, f32[4,16384]{1,0:T(4,128)S(1)}, u32[]{:S(2)}, u32[]{:S(2)}) collective-permute-start(f32[4,16384]{1,0:T(4,128)S(1)} %pad_maximum_fusion.7), channel_id=1, source_target_pairs={{8,0},{16,8},{24,16},{32,24},{40,32},{48,40},{56,48},{64,56},{72,6... | collective-permute-start | bytes 786440 | tf_op jit(solution)/shard_map/while/body/eval_jaxpr/ppermute | solution.py:13
  240.6 10.4 %collective-permute-start = (f32[4,16384]{1,0:T(4,128)S(1)}, f32[4,16384]{1,0:T(4,128)S(1)}, u32[]{:S(2)}, u32[]{:S(2)}) collective-permute-start(f32[4,16384]{1,0:T(4,128)S(1)} %pad_maximum_fusion.7), channel_id=1, source_target_pairs={{8,0},{16,8},{24,16},{32,24},{40,32},{48,40},{56,48},{64,56},{72,6... | collective-permute-start | bytes 786440 | tf_op jit(solution)/shard_map/while/body/eval_jaxpr/ppermute | solution.py:13
  264.3 10.4 %collective-permute-start = (f32[4,16384]{1,0:T(4,128)S(1)}, f32[4,16384]{1,0:T(4,128)S(1)}, u32[]{:S(2)}, u32[]{:S(2)}) collective-permute-start(f32[4,16384]{1,0:T(4,128)S(1)} %pad_maximum_fusion.7), channel_id=1, source_target_pairs={{8,0},{16,8},{24,16},{32,24},{40,32},{48,40},{56,48},{64,56},{72,6... | collective-permute-start | bytes 786440 | tf_op jit(solution)/shard_map/while/body/eval_jaxpr/ppermute | solution.py:13
  299.9 11.2 %collective-permute-start = (f32[4,16384]{1,0:T(4,128)S(1)}, f32[4,16384]{1,0:T(4,128)S(1)}, u32[]{:S(2)}, u32[]{:S(2)}) collective-permute-start(f32[4,16384]{1,0:T(4,128)S(1)} %pad_maximum_fusion.7), channel_id=1, source_target_pairs={{8,0},{16,8},{24,16},{32,24},{40,32},{48,40},{56,48},{64,56},{72,6... | collective-permute-start | bytes 786440 | tf_op jit(solution)/shard_map/while/body/eval_jaxpr/ppermute | solution.py:13
  312.5 12.3 %collective-permute-start = (f32[4,16384]{1,0:T(4,128)S(1)}, f32[4,16384]{1,0:T(4,128)S(1)}, u32[]{:S(2)}, u32[]{:S(2)}) collective-permute-start(f32[4,16384]{1,0:T(4,128)S(1)} %pad_maximum_fusion.7), channel_id=1, source_target_pairs={{8,0},{16,8},{24,16},{32,24},{40,32},{48,40},{56,48},{64,56},{72,6... | collective-permute-start | bytes 786440 | tf_op jit(solution)/shard_map/while/body/eval_jaxpr/ppermute | solution.py:13
  326.3 13.3 %collective-permute-start = (f32[4,16384]{1,0:T(4,128)S(1)}, f32[4,16384]{1,0:T(4,128)S(1)}, u32[]{:S(2)}, u32[]{:S(2)}) collective-permute-start(f32[4,16384]{1,0:T(4,128)S(1)} %pad_maximum_fusion.7), channel_id=1, source_target_pairs={{8,0},{16,8},{24,16},{32,24},{40,32},{48,40},{56,48},{64,56},{72,6... | collective-permute-start | bytes 786440 | tf_op jit(solution)/shard_map/while/body/eval_jaxpr/ppermute | solution.py:13
  341.0 12.4 %collective-permute-start = (f32[4,16384]{1,0:T(4,128)S(1)}, f32[4,16384]{1,0:T(4,128)S(1)}, u32[]{:S(2)}, u32[]{:S(2)}) collective-permute-start(f32[4,16384]{1,0:T(4,128)S(1)} %pad_maximum_fusion.7), channel_id=1, source_target_pairs={{8,0},{16,8},{24,16},{32,24},{40,32},{48,40},{56,48},{64,56},{72,6... | collective-permute-start | bytes 786440 | tf_op jit(solution)/shard_map/while/body/eval_jaxpr/ppermute | solution.py:13
  354.9 11.6 %collective-permute-start = (f32[4,16384]{1,0:T(4,128)S(1)}, f32[4,16384]{1,0:T(4,128)S(1)}, u32[]{:S(2)}, u32[]{:S(2)}) collective-permute-start(f32[4,16384]{1,0:T(4,128)S(1)} %pad_maximum_fusion.7), channel_id=1, source_target_pairs={{8,0},{16,8},{24,16},{32,24},{40,32},{48,40},{56,48},{64,56},{72,6... | collective-permute-start | bytes 786440 | tf_op jit(solution)/shard_map/while/body/eval_jaxpr/ppermute | solution.py:13
  367.9 10.7 %collective-permute-start = (f32[4,16384]{1,0:T(4,128)S(1)}, f32[4,16384]{1,0:T(4,128)S(1)}, u32[]{:S(2)}, u32[]{:S(2)}) collective-permute-start(f32[4,16384]{1,0:T(4,128)S(1)} %pad_maximum_fusion.7), channel_id=1, source_target_pairs={{8,0},{16,8},{24,16},{32,24},{40,32},{48,40},{56,48},{64,56},{72,6... | collective-permute-start | bytes 786440 | tf_op jit(solution)/shard_map/while/body/eval_jaxpr/ppermute | solution.py:13
  443.1 43.8 %all-to-all-start.1 = ((f32[8,32,2,128]{3,2,1,0:T(2,128)}), f32[8,32,2,128]{3,2,1,0:T(2,128)S(1)}, u32[]{:S(2)}, u32[]{:S(2)}) async-start(f32[8,32,2,128]{3,2,1,0:T(2,128)} %bitcast.21), calls=%async_computation.1 | async-start | bytes 524288 | tf_op jit(solution)/shard_map/all_to_all | solution.py:97
  (18 other events, 148.5 us)
